TPU v7x, 32 devices: a whole 2x2x4 slice. The times are simulated.
32 devices in a mesh: tm: 16 (over z, y, x), tensor: 2 (over core).
Axes of the slice: x: 2, y: 2, z: 4, core: 2. Of those that a mesh axis runs over, the one named last changes fastest.
Arguments:
- noise_start: float32 [1, 16384], replicated, may hold values from -6 to 6
- timesteps: int32 [17], replicated, may hold values from 0 to 599, as said below
- class_labels: int32 [16, 1], P('tm'), may hold values from 0 to 999
- mixing: float32 [2, 16], P(None, 'tm'), may hold values from -0.5 to 0.5
- class_table: bfloat16 [1000, 768], replicated, may hold values from -3 to 3
- time_in: bfloat16 [256, 768], replicated, may hold values from -0.75 to 0.75
- time_out: bfloat16 [768, 768], replicated, may hold values from -0.21875 to 0.21875
- ada_weight: bfloat16 [768, 4608], replicated, may hold values from -0.21875 to 0.21875
- final_ada: bfloat16 [768, 1536], replicated, may hold values from -0.21875 to 0.21875
- patch_weight: bfloat16 [16, 768], replicated, may hold values from -1.5 to 1.5
- q_weight: bfloat16 [768, 768], replicated, may hold values from -1.5 to 1.5
- kv_weight: bfloat16 [768, 1536], replicated, may hold values from -1.5 to 1.5
- out_weight: bfloat16 [768, 768], replicated, may hold values from -0.4375 to 0.4375
- up_weight: bfloat16 [768, 3072], P(None, 'tensor'), may hold values from -0.21875 to 0.21875
- down_weight: bfloat16 [3072, 768], P('tensor'), may hold values from -0.21875 to 0.21875
- final_weight: bfloat16 [768, 16], replicated, may hold values from -0.21875 to 0.21875
Outputs:
- states: float32 [16, 1, 16384], P('tm')
- residuals: float32 [2, 16], P(None, 'tm')
Inputs may be any that keep to these rules, and one draw needn't show every extreme that they name: `timesteps`: strictly decreasing; the first is 599, the last is 0, all others lie from 100 to 549.
All inputs are finite; a program needn't handle non-finite values.
Results may differ from a plain program's by a relative error of at most 0.008.
Values may be sent and summed in bfloat16 or wider, within the bound.
A program may use at most 128 MiB of HBM per device.

v0:
```python
import math
import jax
import jax.numpy as jnp
from jax import lax
from jax.sharding import PartitionSpec as P

D = 768
HEADS = 12
SEQ = 1024
PATCH = 16
CLASSES = 1000
FREQ = 256
IMG = 1
ITERS = 2
LAT = 16384
norm_eps = 1e-06
plan_steps = 1000


def prefix(array, axis, combine, identity):
    size, here = (lax.axis_size(axis), lax.axis_index(axis))
    everything = lax.all_gather(
        array.astype(jnp.bfloat16 if array.dtype == jnp.float32 else array.dtype), axis
    )
    start = jnp.broadcast_to(jnp.asarray(identity, array.dtype), array.shape)

    def step(k, before):
        reached = k < here
        new = combine(before, everything[k].astype(array.dtype))
        return jnp.where(reached, new, before)

    return lax.fori_loop(0, size, step, start)


def shortened(array):
    return jax.tree.map(lambda a: a.astype(jnp.bfloat16) if a.dtype == jnp.float32 else a, array)


def from_behind(value, axis, steps):
    count = lax.axis_size(axis)
    leading, last = (max(0, -steps), min(count, count - steps))
    return lax.ppermute(value, axis, [(source, source + steps) for source in range(leading, last)])


def log_table():
    levels = jnp.arange(plan_steps, dtype=jnp.float32)
    beta_values = 0.0001 + (0.02 - 0.0001) * levels / (plan_steps - 1)
    return jnp.cumsum(jnp.log(1.0 - beta_values))


def alpha_at(moments):
    matches = moments[:, None] == jnp.arange(plan_steps, dtype=jnp.int32)[None, :]
    return jnp.exp(jnp.sum(jnp.where(matches, log_table()[None, :], 0.0), axis=1))


def time_features(moment):
    half_count = FREQ // 2
    freq_rates = jnp.exp(
        -math.log(10000.0) * jnp.arange(half_count, dtype=jnp.float32) / half_count
    )
    angles = moment.astype(jnp.float32) * freq_rates
    return jnp.concatenate([jnp.cos(angles), jnp.sin(angles)])[None, :]


def positions():
    half_width = D // 2
    places = jnp.arange(SEQ, dtype=jnp.float32)[:, None]
    freq_rates = jnp.exp(
        -math.log(10000.0) * jnp.arange(half_width, dtype=jnp.float32) / half_width
    )
    angles = places * freq_rates[None, :]
    return jnp.concatenate([jnp.sin(angles), jnp.cos(angles)], axis=1)


def layer_norm(values):
    center = values - jnp.mean(values, axis=-1, keepdims=True)
    spread = jnp.mean(center * center, axis=-1, keepdims=True)
    return center * lax.rsqrt(spread + norm_eps)


def modulate(values, shift, scale):
    return layer_norm(values) * (1.0 + scale) + shift


def split_rows(matrix, count):
    return [matrix[:, None, column * D : (column + 1) * D] for column in range(count)]


def add_fields(earlier, later_part):
    return earlier + later_part


def pick_entry(vector, wanted):
    matches = jnp.arange(vector.shape[0], dtype=jnp.int32) == wanted
    return jnp.sum(jnp.where(matches, vector, 0))


def per_device(
    noise_start,
    timesteps,
    class_labels,
    mixing,
    class_table,
    time_in,
    time_out,
    ada_weight,
    final_ada,
    patch_weight,
    q_weight,
    kv_weight,
    out_weight,
    up_weight,
    down_weight,
    final_weight,
):
    window_point = lax.axis_index("tm")
    group_size = lax.axis_size("tensor")
    member = lax.axis_index("tensor")
    rows_own = SEQ // group_size
    offset = member * rows_own
    head_dim = D // HEADS
    moment_now = pick_entry(timesteps, window_point)
    moment_next = pick_entry(timesteps, window_point + 1)
    alphas = alpha_at(jnp.stack([moment_now, moment_next]))
    keep_coef = jnp.sqrt(alphas[1] / alphas[0])
    noise_coef = jnp.sqrt(1.0 - alphas[1]) - jnp.sqrt(alphas[1] * (1.0 - alphas[0]) / alphas[0])
    features = time_features(moment_now).astype(jnp.bfloat16)
    time_hidden = jax.nn.silu(
        jnp.dot(features, time_in, preferred_element_type=jnp.float32)
    ).astype(jnp.bfloat16)
    time_embed = jnp.dot(time_hidden, time_out, preferred_element_type=jnp.float32)
    onehot = (class_labels[0][:, None] == jnp.arange(CLASSES, dtype=jnp.int32)[None, :]).astype(
        jnp.bfloat16
    )
    classes = jnp.dot(onehot, class_table, preferred_element_type=jnp.float32)
    summed = jax.nn.silu(time_embed + classes).astype(jnp.bfloat16)
    modul = jnp.dot(summed, ada_weight, preferred_element_type=jnp.float32)
    final_mod = jnp.dot(summed, final_ada, preferred_element_type=jnp.float32)
    shift_attn, scale_attn, gate_attn, shift_mlp, scale_mlp, gate_mlp = split_rows(modul, 6)
    shift_out, scale_out = split_rows(final_mod, 2)
    place_rows = lax.dynamic_slice_in_dim(positions(), offset, rows_own, 0)
    state_in = noise_start
    state_out = noise_start
    previous = noise_start
    residual_rows = []
    for iteration in range(ITERS):
        tokens = state_in.astype(jnp.bfloat16).reshape(IMG, SEQ, PATCH)
        own_tokens = lax.dynamic_slice_in_dim(tokens, offset, rows_own, 1).reshape(
            IMG * rows_own, PATCH
        )
        hidden = jnp.dot(own_tokens, patch_weight, preferred_element_type=jnp.float32).reshape(
            IMG, rows_own, D
        )
        hidden = hidden + place_rows[None]
        attn_in = (
            modulate(hidden, shift_attn, scale_attn).astype(jnp.bfloat16).reshape(IMG * rows_own, D)
        )
        queries = jnp.dot(attn_in, q_weight, preferred_element_type=jnp.float32).astype(
            jnp.bfloat16
        )
        queries = queries.reshape(IMG, rows_own, HEADS, head_dim)
        key_value = jnp.dot(attn_in, kv_weight, preferred_element_type=jnp.float32).astype(
            jnp.bfloat16
        )
        key_value = key_value.reshape(IMG, rows_own, 2 * D)
        gathered = lax.all_gather(key_value, "tensor", axis=1, tiled=True)
        key_heads = gathered[:, :, :D].reshape(IMG, SEQ, HEADS, head_dim)
        value_heads = gathered[:, :, D:].reshape(IMG, SEQ, HEADS, head_dim)
        scores = jnp.einsum(
            "bqhd,bkhd->bhqk", queries, key_heads, preferred_element_type=jnp.float32
        )
        scores = scores * (1.0 / math.sqrt(head_dim))
        attention = jax.nn.softmax(scores, axis=-1).astype(jnp.bfloat16)
        attended = jnp.einsum(
            "bhqk,bkhd->bqhd", attention, value_heads, preferred_element_type=jnp.float32
        )
        attended = attended.astype(jnp.bfloat16).reshape(IMG * rows_own, D)
        projected = jnp.dot(attended, out_weight, preferred_element_type=jnp.float32).reshape(
            IMG, rows_own, D
        )
        hidden = hidden + gate_attn * projected
        stream = lax.all_gather(hidden.astype(jnp.bfloat16), "tensor", axis=1, tiled=True).astype(
            hidden.dtype
        )
        predict_mlp_in = modulate(stream, shift_mlp, scale_mlp).astype(jnp.bfloat16)
        flat_in = predict_mlp_in.reshape(IMG * SEQ, D)
        lifted = jax.nn.gelu(
            jnp.dot(flat_in, up_weight, preferred_element_type=jnp.float32), approximate=True
        )
        lifted = lifted.astype(jnp.bfloat16)
        mlp_sum = lax.psum(
            jnp.dot(lifted, down_weight, preferred_element_type=jnp.float32)
            .reshape(IMG, SEQ, D)
            .astype(jnp.bfloat16),
            "tensor",
        ).astype(jnp.float32)
        stream_out = stream + gate_mlp * mlp_sum
        final_in = (
            modulate(stream_out, shift_out, scale_out).astype(jnp.bfloat16).reshape(IMG * SEQ, D)
        )
        predicted = jnp.dot(final_in, final_weight, preferred_element_type=jnp.float32).reshape(
            IMG, LAT
        )
        drift_now = (keep_coef - 1.0) * state_in + noise_coef * predicted
        slice_width = LAT // group_size
        drift_piece = lax.dynamic_slice_in_dim(drift_now, member * slice_width, slice_width, 1)
        before_piece = prefix(drift_piece, "tm", add_fields, jnp.zeros_like(drift_piece))
        reached = lax.all_gather(
            shortened(before_piece + drift_piece), "tensor", axis=1, tiled=True
        )
        picard_map = noise_start + reached
        residual_rows.append(jnp.mean(jnp.square(picard_map - state_out)))
        state_new = picard_map + mixing[iteration, 0] * (picard_map - previous)
        previous = picard_map
        state_out = state_new
        if iteration + 1 < ITERS:
            state_in = noise_start + from_behind(shortened(state_new - noise_start), "tm", 1)
    return (state_out[None], jnp.stack(residual_rows)[:, None])


def solution(mesh):
    in_specs = (
        P(),
        P(),
        P("tm", None),
        P(None, "tm"),
        P(),
        P(),
        P(),
        P(),
        P(),
        P(),
        P(),
        P(),
        P(),
        P(None, "tensor"),
        P("tensor", None),
        P(),
    )
    out_specs = (P("tm", None, None), P(None, "tm"))
    return jax.shard_map(
        per_device, mesh=mesh, in_specs=in_specs, out_specs=out_specs, check_vma=False
    )
```

profile of v0, /device:TPU:0, one launch (start us, length us, event | category | flops | bytes accessed | tf_op | source)
XLA Modules:
  0.0 339.4 jit_solution(7551914350179567751)
XLA Ops:
  7.3 6.6 %fusion.78 = (f32[1024,384]{1,0:T(8,128)}, f32[1024,384]{1,0:T(8,128)}) fusion(f32[384]{0:T(512)S(1)} %multiply_exponential_fusion), kind=kLoop, calls=%fused_computation.95 | loop fusion | flops 393216 | bytes 3147264 | tf_op jit(solution)/shard_map/sin | solution.py:72
  23.3 4.1 %fusion.135 = f32[1,4608]{1,0:T(1,128)S(1)} fusion(bf16[768,1]{0,1:T(2,128)(2,1)S(1)} %reshape.487, bf16[768,4608]{1,0:T(8,128)(2,1)} %param.27), kind=kOutput, calls=%fused_computation.196 | convolution fusion | flops 7077888 | bytes 7097856 | tf_op jit(solution)/shard_map/dot_general | solution.py:137
  27.6 2.7 convolution_convert_fusion.1
  30.6 3.6 %convolution_convert_fusion.3 = bf16[512,768]{1,0:T(8,128)(2,1)} fusion(bf16[768,768]{1,0:T(8,128)(2,1)} %param.30, f32[512,768]{1,0:T(8,128)} %copy-done.6, f32[768]{0:T(1024)S(1)} %get-tuple-element.196, f32[768]{0:T(1024)S(1)} %get-tuple-element.197, f32[512]{0:T(512)S(1)} %add_rsqrt_fusion.5, f32[512]{0:T(512)S(1)} %broadcast_multiply_fusion.5), kind=kOutput, calls=%fused_computation.105 | convolution fusion | flops 606339072 | bytes 3549184 | tf_op jit(solution)/shard_map/dot_general | solution.py:158
  34.2 2.3 copy.41
  36.5 8.7 %all-gather.13.cloned.1.call-done = bf16[1024,1536]{1,0:T(8,128)(2,1)} async-done(((bf16[512,1536]{1,0:T(8,128)(2,1)}), bf16[1024,1536]{1,0:T(8,128)(2,1)}) %all-gather.13.cloned.1.call-update) | async-done | bytes 3145744 | tf_op jit(solution)/shard_map/all_gather | solution.py:166
  45.2 3.8 %fusion.128 = (bf16[1,1024,768]{2,1,0:T(8,128)(2,1)}, bf16[1,1024,768]{2,1,0:T(8,128)(2,1)}) fusion(bf16[1,1024,1536]{2,1,0:T(8,128)(2,1)} %bitcast.198), kind=kLoop, calls=%fused_computation.189 | loop fusion | bytes 6291456 | tf_op jit(solution)/shard_map/slice | solution.py:167
  49.0 2.6 copy.42
  51.6 2.6 copy.40
  54.2 13.0 %fusion.132 = (f32[12,512]{1,0:T(8,128)S(1)}, f32[12,512,1024]{2,1,0:T(8,128)}) fusion(bf16[512,12,64]{0,2,1:T(8,128)(2,1)} %bitcast.203, bf16[1024,12,64]{0,2,1:T(8,128)(2,1)} %bitcast.199), kind=kOutput, calls=%fused_computation.193 | convolution fusion | flops 824181760 | bytes 27549696 | tf_op jit(solution)/shard_map/sub | solution.py:173
  67.2 10.9 %fusion.90 = bf16[12,64,512]{2,1,0:T(8,128)(2,1)S(1)} fusion(bf16[1024,12,64]{0,2,1:T(8,128)(2,1)} %bitcast.200, f32[12,512,1024]{2,1,0:T(8,128)} %get-tuple-element.240, f32[12,512]{1,0:T(8,128)S(1)} %get-tuple-element.239), kind=kOutput, calls=%fused_computation.103 | convolution fusion | flops 818282496 | bytes 27549696 | tf_op jit(solution)/shard_map/bhqk,bkhd->bqhd/dot_general | solution.py:174
  80.5 10.6 %all-gather.15.cloned.1.call-done = bf16[1024,768]{1,0:T(8,128)(2,1)} async-done(((bf16[512,768]{1,0:T(8,128)(2,1)}), bf16[1024,768]{1,0:T(8,128)(2,1)}) %all-gather.15.cloned.1.call-update) | async-done | bytes 1572880 | tf_op jit(solution)/shard_map/all_gather | solution.py:182
  93.6 9.4 %fusion.86 = bf16[1,1024,768]{2,1,0:T(8,128)(2,1)} fusion(bf16[1536,768]{1,0:T(8,128)(2,1)} %param.34, bf16[768,1536]{1,0:T(8,128)(2,1)} %param.33, bf16[1024,768]{1,0:T(8,128)(2,1)} %all-gather.15.cloned.1.call-done, f32[768]{0:T(1024)S(1)} %get-tuple-element.199, f32[768]{0:T(1024)S(1)} %get-tuple-element.195, f32[1024]{0:T(1024)S(1)} %add_rsqrt_fusion.3, ...), kind=kOutput, calls=%fused_computation.99 | convolution fusion | flops 4851499008 | bytes 7878656 | tf_op jit(solution)/shard_map/dot_general | solution.py:192
  110.2 2.1 fusion.136
  112.4 12.3 %all-reduce.4.cloned.1.call-done = bf16[1,1024,768]{2,1,0:T(8,128)(2,1)} async-done(((bf16[1,1024,768]{2,1,0:T(8,128)(2,1)}), bf16[1,1024,768]{2,1,0:T(8,128)(2,1)}) %all-reduce.4.cloned.1.call-update) | async-done | bytes 1572880 | tf_op jit(solution)/shard_map/psum | solution.py:191
  124.7 2.6 fusion.59
  130.0 44.0 %all-gather.6 = bf16[16,1,8192]{2,1,0:T(2,128)(2,1)S(1)} all-gather(bf16[1,1,8192]{2,1,0:T(2,128)(2,1)S(1)} %get-tuple-element.224), channel_id=4, replica_groups=mesh['tm'=16,'tensor'=2] {'tm'}, dimensions={0}, use_global_device_ids=true | all-gather | bytes 278528 | tf_op jit(solution)/shard_map/all_gather | solution.py:22
  175.4 1.9 all_gather.34
  179.2 1.9 collective-permute-done
  184.6 2.7 convolution_convert_fusion
  187.5 2.7 convolution_convert_fusion.2
  190.5 7.5 %all-gather.17.cloned.1.call-done = bf16[1024,1536]{1,0:T(8,128)(2,1)} async-done(((bf16[512,1536]{1,0:T(8,128)(2,1)}), bf16[1024,1536]{1,0:T(8,128)(2,1)}) %all-gather.17.cloned.1.call-update) | async-done | bytes 3145744 | tf_op jit(solution)/shard_map/all_gather | solution.py:166
  198.0 3.2 fusion.127
  201.2 2.6 copy.46
  205.4 12.9 %fusion.134 = (f32[12,512]{1,0:T(8,128)S(1)}, f32[12,512,1024]{2,1,0:T(8,128)}) fusion(bf16[512,12,64]{0,2,1:T(8,128)(2,1)S(1)} %bitcast.204, bf16[1024,12,64]{0,2,1:T(8,128)(2,1)} %bitcast.201), kind=kOutput, calls=%fused_computation.195 | convolution fusion | flops 824181760 | bytes 27549696 | tf_op jit(solution)/shard_map/sub | solution.py:173
  218.3 10.9 %fusion.89 = bf16[12,64,512]{2,1,0:T(8,128)(2,1)S(1)} fusion(bf16[1024,12,64]{0,2,1:T(8,128)(2,1)} %bitcast.202, f32[12,512,1024]{2,1,0:T(8,128)} %get-tuple-element.244, f32[12,512]{1,0:T(8,128)S(1)} %get-tuple-element.243), kind=kOutput, calls=%fused_computation.102 | convolution fusion | flops 818282496 | bytes 27549696 | tf_op jit(solution)/shard_map/bhqk,bkhd->bqhd/dot_general | solution.py:174
  231.3 10.9 %all-gather.19.cloned.1.call-done = bf16[1024,768]{1,0:T(8,128)(2,1)} async-done(((bf16[512,768]{1,0:T(8,128)(2,1)}), bf16[1024,768]{1,0:T(8,128)(2,1)}) %all-gather.19.cloned.1.call-update) | async-done | bytes 1572880 | tf_op jit(solution)/shard_map/all_gather | solution.py:182
  244.6 8.9 %fusion.83 = bf16[1,1024,768]{2,1,0:T(8,128)(2,1)} fusion(bf16[1536,768]{1,0:T(8,128)(2,1)} %param.34, bf16[768,1536]{1,0:T(8,128)(2,1)} %param.33, bf16[1024,768]{1,0:T(8,128)(2,1)S(1)} %copy-done.4, f32[1024]{0:T(1024)S(1)} %add_rsqrt_fusion.1, f32[1024]{0:T(1024)S(1)} %broadcast_multiply_fusion.1, f32[768]{0:T(1024)S(1)} %get-tuple-element.199, ...), kind=kOutput, calls=%fused_computation.98 | convolution fusion | flops 4851499008 | bytes 7878656 | tf_op jit(solution)/shard_map/dot_general | solution.py:192
  253.6 21.7 %all-reduce.6.cloned.1.call-done = bf16[1,1024,768]{2,1,0:T(8,128)(2,1)} async-done(((bf16[1,1024,768]{2,1,0:T(8,128)(2,1)}), bf16[1,1024,768]{2,1,0:T(8,128)(2,1)}) %all-reduce.6.cloned.1.call-update) | async-done | bytes 1572880 | tf_op jit(solution)/shard_map/psum | solution.py:191
  275.3 2.1 fusion.58
  280.4 44.0 %all-gather.7 = bf16[16,1,8192]{2,1,0:T(2,128)(2,1)S(1)} all-gather(bf16[1,1,8192]{2,1,0:T(2,128)(2,1)S(1)} %get-tuple-element.220), channel_id=7, replica_groups=mesh['tm'=16,'tensor'=2] {'tm'}, dimensions={0}, use_global_device_ids=true | all-gather | bytes 278528 | tf_op jit(solution)/shard_map/all_gather | solution.py:22
  327.6 2.7 multiply_reduce_fusion.7
  (162 shorter events, 41.5 us)
Async XLA Ops:
  7.2 20.4 %copy-start = (bf16[768,1536]{1,0:T(8,128)(2,1)S(1)}, bf16[768,1536]{1,0:T(8,128)(2,1)}, u32[]{:S(2)}) copy-start(bf16[768,1536]{1,0:T(8,128)(2,1)} %param.31) | copy-start | bytes 7077892
  7.2 6.7 %copy-start.13 = (f32[1,16384]{1,0:T(1,128)S(1)}, f32[1,16384]{1,0:T(1,128)}, u32[]{:S(2)}) copy-start(f32[1,16384]{1,0:T(1,128)} %param.20) | copy-start | bytes 196612
  7.2 7.1 %copy-start.15 = (bf16[16,768]{1,0:T(8,128)(2,1)S(1)}, bf16[16,768]{1,0:T(8,128)(2,1)}, u32[]{:S(2)}) copy-start(bf16[16,768]{1,0:T(8,128)(2,1)} %param.29) | copy-start | bytes 73732
  7.2 38.0 %all-gather.13.cloned.1.call-start = ((), (), s32[]{:S(2)}) async-start(), calls=%async_computation.2 | async-start | bytes 4718592 | tf_op jit(solution)/shard_map/all_gather | solution.py:166
  14.3 3.4 copy-start.17
  14.3 4.8 %copy-start.14 = (bf16[256,768]{1,0:T(8,128)(2,1)S(1)}, bf16[256,768]{1,0:T(8,128)(2,1)}, u32[]{:S(2)}) copy-start(bf16[256,768]{1,0:T(8,128)(2,1)} %param.25) | copy-start | bytes 1179652
  16.2 1.2 copy-start.6
  23.3 4.2 %copy-start.7 = (f32[512,768]{1,0:T(8,128)S(1)}, f32[512,768]{1,0:T(8,128)}, u32[]{:S(2)}) copy-start(f32[512,768]{1,0:T(8,128)} %copy-done.6) | copy-start | bytes 4718596
  30.2 60.8 %all-gather.15.cloned.1.call-start = ((), (), s32[]{:S(2)}) async-start(), calls=%async_computation.3 | async-start | bytes 2359296 | tf_op jit(solution)/shard_map/all_gather | solution.py:182
  67.2 10.9 %copy-start.8 = (f32[512,768]{1,0:T(8,128)S(1)}, f32[512,768]{1,0:T(8,128)}, u32[]{:S(2)}) copy-start(f32[512,768]{1,0:T(8,128)} %copy-done.6) | copy-start | bytes 4718596
  67.2 10.9 %copy-start.18 = (bf16[768,768]{1,0:T(8,128)(2,1)S(1)}, bf16[768,768]{1,0:T(8,128)(2,1)}, u32[]{:S(2)}) copy-start(bf16[768,768]{1,0:T(8,128)(2,1)} %param.32) | copy-start | bytes 3538948
  79.9 44.8 %all-reduce.4.cloned.1.call-start = ((), (), s32[]{:S(2)}) async-start(), calls=%async_computation | async-start | bytes 3145728 | tf_op jit(solution)/shard_map/psum | solution.py:191
  91.0 1.9 copy-start.2
  93.5 16.1 %copy-start.16 = (f32[2,1]{0,1:T(1,128)S(1)}, f32[2,1]{0,1:T(1,128)}, u32[]{:S(2)}) copy-start(f32[2,1]{0,1:T(1,128)} %param.23) | copy-start | bytes 28
  103.0 95.0 %all-gather.17.cloned.1.call-start = ((), (), s32[]{:S(2)}) async-start(), calls=%async_computation.4 | async-start | bytes 4718592 | tf_op jit(solution)/shard_map/all_gather | solution.py:166
  124.7 2.6 copy-start.3
  124.7 2.8 copy-start.9
  127.3 1.1 copy-start.20
  177.9 3.2 collective-permute-start
  183.4 1.2 copy-start.10
  187.3 54.8 %all-gather.19.cloned.1.call-start = ((), (), s32[]{:S(2)}) async-start(), calls=%async_computation.5 | async-start | bytes 2359296 | tf_op jit(solution)/shard_map/all_gather | solution.py:182
  218.3 10.9 %copy-start.11 = (f32[512,768]{1,0:T(8,128)S(1)}, f32[512,768]{1,0:T(8,128)}, u32[]{:S(2)}) copy-start(f32[512,768]{1,0:T(8,128)} %copy-done.10) | copy-start | bytes 4718596
  218.3 10.9 %copy-start.19 = (bf16[768,768]{1,0:T(8,128)(2,1)S(1)}, bf16[768,768]{1,0:T(8,128)(2,1)}, u32[]{:S(2)}) copy-start(bf16[768,768]{1,0:T(8,128)(2,1)} %param.32) | copy-start | bytes 3538948
  231.0 44.3 %all-reduce.6.cloned.1.call-start = ((), (), s32[]{:S(2)}) async-start(), calls=%async_computation.1 | async-start | bytes 3145728 | tf_op jit(solution)/shard_map/psum | solution.py:191
  242.1 1.9 copy-start.4
  275.3 2.1 copy-start.12
  277.4 1.4 copy-start.5
  278.8 53.5 %copy-start.1 = (bf16[768,1536]{1,0:T(8,128)(2,1)S(1)}, bf16[768,1536]{1,0:T(8,128)(2,1)}, u32[]{:S(2)}) copy-start(bf16[768,1536]{1,0:T(8,128)(2,1)} %param.31) | copy-start | bytes 7077892
Sparse Core Ops, SparseCore 0:
  30.4 14.8 all-gather.12
  80.0 10.9 all-gather.14
  103.1 21.5 all-reduce.3
  187.4 10.4 all-gather.16
  231.1 10.9 all-gather.18
  253.7 21.5 all-reduce.5
where the time goes:
time: 344 us; the launch traced here: 339 us
  matrix products  96.6 us (28%)
  blocking collectives  91.7 us (27%)
  waiting for transfers between devices  73.7 us (21%)
  other arithmetic  27.8 us (8%)
  local copies, waits for them, and re-layouts  24.7 us (7%)
  between operations  21.3 us (6%)
    all_gather x2, blocking collectives, prefix(): lax.all_gather(array.astype(jnp.bfloat16 if array.dtype == jnp.float32 el...  88 us
    psum x2, waiting for transfers between devices, per_device(): lax.psum(jnp.dot(lifted, down_weight, preferred_element_type=jnp.float32)...  34 us
    sub x2, matrix products, per_device(): attention = jax.nn.softmax(scores, axis=-1).astype(jnp.bfloat16)  25.9 us
    dot_general x2, matrix products, per_device(): jnp.einsum('bhqk,bkhd->bqhd', attention, value_heads, preferred_element_t...  21.8 us
    all_gather x2, waiting for transfers between devices, per_device(): lax.all_gather(hidden.astype(jnp.bfloat16), 'tensor', axis=1, tiled=True)  21.4 us
    dot_general x2, matrix products, per_device(): jnp.dot(lifted, down_weight, preferred_element_type=jnp.float32)  18.3 us
    all_gather x2, waiting for transfers between devices, per_device(): gathered = lax.all_gather(key_value, 'tensor', axis=1, tiled=True)  16.2 us
    slice x4, local copies, waits for them, and re-layouts, per_device(): key_heads = gathered[:, :, :D].reshape(IMG, SEQ, HEADS, head_dim)  12.2 us
  transfers between devices with their start and end apart: 7, of which 7 were waited for; matrix products, arithmetic and copies ran while one was open for 4% of the time, Pallas kernels for 0%

commit v1 on v0

--- a/solution.py
+++ b/solution.py
@@ -179,9 +179,12 @@
             IMG, rows_own, D
         )
         hidden = hidden + gate_attn * projected
-        stream = lax.all_gather(hidden.astype(jnp.bfloat16), "tensor", axis=1, tiled=True).astype(
-            hidden.dtype
-        )
+        stream = jnp.concatenate(
+            lax.all_to_all(
+                jnp.stack([hidden.astype(jnp.bfloat16)] * lax.axis_size("tensor")), "tensor", 0, 0
+            ),
+            axis=1,
+        ).astype(hidden.dtype)
         predict_mlp_in = modulate(stream, shift_mlp, scale_mlp).astype(jnp.bfloat16)
         flat_in = predict_mlp_in.reshape(IMG * SEQ, D)
         lifted = jax.nn.gelu(

time: 344 us -> 336 us (0.977)
  waiting for transfers between devices: 73.7 us -> 52.2 us
  blocking collectives: 91.7 us -> 102 us
  other arithmetic: 27.8 us -> 32.9 us
    all_gather x2 -> x0, waiting for transfers between devices: 21.4 us -> none  [per_device(): lax.all_gather(hidden.astype(jnp.bfloat16), 'tensor', axis=1, tiled=True)]
    all_to_all x0 -> x2, blocking collectives: none -> 10.7 us  [per_device(): lax.all_to_all(jnp.stack([hidden.astype(jnp.bfloat16)] * lax.axis_size('t...]
    convert_element_type x0 -> x2, other arithmetic: none -> 3.55 us  [per_device(): predict_mlp_in = modulate(stream, shift_mlp, scale_mlp).astype(jnp.bfloat16)]
  transfers between devices with their start and end apart: 7 -> 5, of which waited for: 7 -> 5; matrix products, arithmetic and copies ran while one was open for 4% -> 4% of each run, Pallas kernels for 0% -> 0%
where the time goes in v1:
time: 336 us; the launch traced here: 331 us
  blocking collectives  102 us (30%)
  matrix products  94.9 us (28%)
  waiting for transfers between devices  52.2 us (16%)
  other arithmetic  32.9 us (10%)
  local copies, waits for them, and re-layouts  25.4 us (8%)
  between operations  21 us (6%)
    all_gather x2, blocking collectives, prefix(): lax.all_gather(array.astype(jnp.bfloat16 if array.dtype == jnp.float32 el...  88 us
    psum x2, waiting for transfers between devices, per_device(): lax.psum(jnp.dot(lifted, down_weight, preferred_element_type=jnp.float32)...  34 us
    sub x2, matrix products, per_device(): attention = jax.nn.softmax(scores, axis=-1).astype(jnp.bfloat16)  25.9 us
    dot_general x2, matrix products, per_device(): jnp.einsum('bhqk,bkhd->bqhd', attention, value_heads, preferred_element_t...  21.8 us
    dot_general x2, matrix products, per_device(): jnp.dot(lifted, down_weight, preferred_element_type=jnp.float32)  18.6 us
    all_gather x2, waiting for transfers between devices, per_device(): gathered = lax.all_gather(key_value, 'tensor', axis=1, tiled=True)  16.2 us
    slice x4, local copies, waits for them, and re-layouts, per_device(): key_heads = gathered[:, :, :D].reshape(IMG, SEQ, HEADS, head_dim)  12.2 us
    all_to_all x2, blocking collectives, per_device(): lax.all_to_all(jnp.stack([hidden.astype(jnp.bfloat16)] * lax.axis_size('t...  10.7 us
  transfers between devices with their start and end apart: 5, of which 5 were waited for; matrix products, arithmetic and copies ran while one was open for 4% of the time, Pallas kernels for 0%

profile of v1, /device:TPU:0, one launch (start us, length us, event | category | flops | bytes accessed | tf_op | source)
XLA Modules:
  0.0 331.5 jit_solution(14280559630135858034)
XLA Ops:
  7.3 6.6 %fusion.54 = (f32[1024,384]{1,0:T(8,128)}, f32[1024,384]{1,0:T(8,128)}) fusion(f32[384]{0:T(512)S(1)} %multiply_exponential_fusion), kind=kLoop, calls=%fused_computation.77 | loop fusion | flops 393216 | bytes 3147264 | tf_op jit(solution)/shard_map/sin | solution.py:72
  23.3 4.1 %fusion.111 = f32[1,4608]{1,0:T(1,128)S(1)} fusion(bf16[768,1]{0,1:T(2,128)(2,1)S(1)} %reshape.669, bf16[768,4608]{1,0:T(8,128)(2,1)} %param.27), kind=kOutput, calls=%fused_computation.186 | convolution fusion | flops 7077888 | bytes 7097856 | tf_op jit(solution)/shard_map/dot_general | solution.py:137
  27.6 2.7 convolution_convert_fusion.1
  30.6 3.6 %convolution_convert_fusion.3 = bf16[512,768]{1,0:T(8,128)(2,1)} fusion(bf16[768,768]{1,0:T(8,128)(2,1)} %param.30, f32[512,768]{1,0:T(8,128)} %copy-done.4, f32[768]{0:T(1024)S(1)} %get-tuple-element.196, f32[768]{0:T(1024)S(1)} %get-tuple-element.197, f32[512]{0:T(512)S(1)} %add_rsqrt_fusion.5, f32[512]{0:T(512)S(1)} %broadcast_multiply_fusion.3), kind=kOutput, calls=%fused_computation.87 | convolution fusion | flops 606339072 | bytes 3549184 | tf_op jit(solution)/shard_map/dot_general | solution.py:158
  34.2 2.3 copy.41
  36.5 8.7 %all-gather.9.cloned.1.call-done = bf16[1024,1536]{1,0:T(8,128)(2,1)} async-done(((bf16[512,1536]{1,0:T(8,128)(2,1)}), bf16[1024,1536]{1,0:T(8,128)(2,1)}) %all-gather.9.cloned.1.call-update) | async-done | bytes 3145744 | tf_op jit(solution)/shard_map/all_gather | solution.py:166
  45.2 3.8 %fusion.100 = (bf16[1,1024,768]{2,1,0:T(8,128)(2,1)}, bf16[1,1024,768]{2,1,0:T(8,128)(2,1)}) fusion(bf16[1,1024,1536]{2,1,0:T(8,128)(2,1)} %bitcast.150), kind=kLoop, calls=%fused_computation.177 | loop fusion | bytes 6291456 | tf_op jit(solution)/shard_map/slice | solution.py:167
  49.0 2.6 copy.42
  51.6 2.6 copy.40
  54.2 13.0 %fusion.104 = (f32[12,512]{1,0:T(8,128)S(1)}, f32[12,512,1024]{2,1,0:T(8,128)}) fusion(bf16[512,12,64]{0,2,1:T(8,128)(2,1)} %bitcast.155, bf16[1024,12,64]{0,2,1:T(8,128)(2,1)} %bitcast.151), kind=kOutput, calls=%fused_computation.181 | convolution fusion | flops 824181760 | bytes 27549696 | tf_op jit(solution)/shard_map/sub | solution.py:173
  67.2 10.9 %fusion.66 = bf16[12,64,512]{2,1,0:T(8,128)(2,1)S(1)} fusion(bf16[1024,12,64]{0,2,1:T(8,128)(2,1)} %bitcast.152, f32[12,512,1024]{2,1,0:T(8,128)} %get-tuple-element.244, f32[12,512]{1,0:T(8,128)S(1)} %get-tuple-element.243), kind=kOutput, calls=%fused_computation.85 | convolution fusion | flops 818282496 | bytes 27549696 | tf_op jit(solution)/shard_map/bhqk,bkhd->bqhd/dot_general | solution.py:174
  79.1 5.5 %all_to_all.10 = bf16[2,1,512,768]{3,2,1,0:T(8,128)(2,1)S(1)} all-to-all(bf16[2,1,512,768]{3,2,1,0:T(8,128)(2,1)S(1)} %pad_maximum_fusion), channel_id=1, replica_groups=mesh['tm'=16,'tensor'=2] {'tensor'}, dimensions={0} | all-to-all | bytes 3145728 | tf_op jit(solution)/shard_map/all_to_all | solution.py:183
  84.9 2.2 multiply_reduce_fusion.5
  88.9 9.3 %fusion.62 = bf16[1,1024,768]{2,1,0:T(8,128)(2,1)} fusion(bf16[1536,768]{1,0:T(8,128)(2,1)} %param.34, bf16[1024,768]{1,0:T(8,128)(2,1)} %fusion.35, bf16[768,1536]{1,0:T(8,128)(2,1)} %param.33), kind=kOutput, calls=%fused_computation.81 | convolution fusion | flops 4846780416 | bytes 7864320 | tf_op jit(solution)/shard_map/dot_general | solution.py:195
  105.5 2.1 fusion.112
  107.7 12.3 %all-reduce.4.cloned.1.call-done = bf16[1,1024,768]{2,1,0:T(8,128)(2,1)} async-done(((bf16[1,1024,768]{2,1,0:T(8,128)(2,1)}), bf16[1,1024,768]{2,1,0:T(8,128)(2,1)}) %all-reduce.4.cloned.1.call-update) | async-done | bytes 1572880 | tf_op jit(solution)/shard_map/psum | solution.py:194
  119.9 3.0 fusion.75
  126.1 44.0 %all-gather.4 = bf16[16,1,8192]{2,1,0:T(2,128)(2,1)S(1)} all-gather(bf16[1,1,8192]{2,1,0:T(2,128)(2,1)S(1)} %get-tuple-element.226), channel_id=3, replica_groups=mesh['tm'=16,'tensor'=2] {'tm'}, dimensions={0}, use_global_device_ids=true | all-gather | bytes 278528 | tf_op jit(solution)/shard_map/all_gather | solution.py:22
  180.7 2.7 convolution_convert_fusion
  183.6 2.7 convolution_convert_fusion.2
  186.5 7.5 %all-gather.11.cloned.1.call-done = bf16[1024,1536]{1,0:T(8,128)(2,1)} async-done(((bf16[512,1536]{1,0:T(8,128)(2,1)}), bf16[1024,1536]{1,0:T(8,128)(2,1)}) %all-gather.11.cloned.1.call-update) | async-done | bytes 3145744 | tf_op jit(solution)/shard_map/all_gather | solution.py:166
  194.0 3.2 fusion.99
  197.2 2.6 copy.46
  201.5 12.9 %fusion.106 = (f32[12,512]{1,0:T(8,128)S(1)}, f32[12,512,1024]{2,1,0:T(8,128)}) fusion(bf16[512,12,64]{0,2,1:T(8,128)(2,1)S(1)} %bitcast.156, bf16[1024,12,64]{0,2,1:T(8,128)(2,1)} %bitcast.153), kind=kOutput, calls=%fused_computation.183 | convolution fusion | flops 824181760 | bytes 27549696 | tf_op jit(solution)/shard_map/sub | solution.py:173
  214.4 10.9 %fusion.65 = bf16[12,64,512]{2,1,0:T(8,128)(2,1)S(1)} fusion(bf16[1024,12,64]{0,2,1:T(8,128)(2,1)} %bitcast.154, f32[12,512,1024]{2,1,0:T(8,128)} %get-tuple-element.248, f32[12,512]{1,0:T(8,128)S(1)} %get-tuple-element.247), kind=kOutput, calls=%fused_computation.84 | convolution fusion | flops 818282496 | bytes 27549696 | tf_op jit(solution)/shard_map/bhqk,bkhd->bqhd/dot_general | solution.py:174
  226.3 5.2 %all_to_all.11 = bf16[2,1,512,768]{3,2,1,0:T(8,128)(2,1)S(1)} all-to-all(bf16[2,1,512,768]{3,2,1,0:T(8,128)(2,1)S(1)} %pad_maximum_fusion.1), channel_id=1, replica_groups=mesh['tm'=16,'tensor'=2] {'tensor'}, dimensions={0} | all-to-all | bytes 3145728 | tf_op jit(solution)/shard_map/all_to_all | solution.py:183
  231.8 2.2 multiply_reduce_fusion.3
  235.7 9.3 %fusion.59 = bf16[1,1024,768]{2,1,0:T(8,128)(2,1)} fusion(bf16[1536,768]{1,0:T(8,128)(2,1)} %param.34, bf16[1024,768]{1,0:T(8,128)(2,1)} %fusion.31, bf16[768,1536]{1,0:T(8,128)(2,1)} %param.33), kind=kOutput, calls=%fused_computation.80 | convolution fusion | flops 4846780416 | bytes 7864320 | tf_op jit(solution)/shard_map/dot_general | solution.py:195
  245.0 21.7 %all-reduce.6.cloned.1.call-done = bf16[1,1024,768]{2,1,0:T(8,128)(2,1)} async-done(((bf16[1,1024,768]{2,1,0:T(8,128)(2,1)}), bf16[1,1024,768]{2,1,0:T(8,128)(2,1)}) %all-reduce.6.cloned.1.call-update) | async-done | bytes 1572880 | tf_op jit(solution)/shard_map/psum | solution.py:194
  266.7 3.0 fusion.76
  272.8 44.0 %all-gather.5 = bf16[16,1,8192]{2,1,0:T(2,128)(2,1)S(1)} all-gather(bf16[1,1,8192]{2,1,0:T(2,128)(2,1)S(1)} %get-tuple-element.220), channel_id=5, replica_groups=mesh['tm'=16,'tensor'=2] {'tm'}, dimensions={0}, use_global_device_ids=true | all-gather | bytes 278528 | tf_op jit(solution)/shard_map/all_gather | solution.py:22
  320.1 2.7 multiply_reduce_fusion.9
  (160 shorter events, 42.5 us)
Async XLA Ops:
  7.2 20.4 %copy-start = (bf16[768,1536]{1,0:T(8,128)(2,1)S(1)}, bf16[768,1536]{1,0:T(8,128)(2,1)}, u32[]{:S(2)}) copy-start(bf16[768,1536]{1,0:T(8,128)(2,1)} %param.31) | copy-start | bytes 7077892
  7.2 6.7 %copy-start.11 = (f32[1,16384]{1,0:T(1,128)S(1)}, f32[1,16384]{1,0:T(1,128)}, u32[]{:S(2)}) copy-start(f32[1,16384]{1,0:T(1,128)} %param.20) | copy-start | bytes 196612
  7.2 7.1 %copy-start.13 = (bf16[16,768]{1,0:T(8,128)(2,1)S(1)}, bf16[16,768]{1,0:T(8,128)(2,1)}, u32[]{:S(2)}) copy-start(bf16[16,768]{1,0:T(8,128)(2,1)} %param.29) | copy-start | bytes 73732
  7.2 38.0 %all-gather.9.cloned.1.call-start = ((), (), s32[]{:S(2)}) async-start(), calls=%async_computation.4 | async-start | bytes 4718592 | tf_op jit(solution)/shard_map/all_gather | solution.py:166
  14.3 3.4 %copy-start.15 = (s32[17]{0:T(128)S(1)}, s32[17]{0:T(128)}, u32[]{:S(2)}) copy-start(s32[17]{0:T(128)} %param.21) | copy-start | bytes 208
  14.3 4.8 %copy-start.12 = (bf16[256,768]{1,0:T(8,128)(2,1)S(1)}, bf16[256,768]{1,0:T(8,128)(2,1)}, u32[]{:S(2)}) copy-start(bf16[256,768]{1,0:T(8,128)(2,1)} %param.25) | copy-start | bytes 1179652
  16.2 1.2 copy-start.4
  23.3 4.2 %copy-start.5 = (f32[512,768]{1,0:T(8,128)S(1)}, f32[512,768]{1,0:T(8,128)}, u32[]{:S(2)}) copy-start(f32[512,768]{1,0:T(8,128)} %copy-done.4) | copy-start | bytes 4718596
  30.2 89.7 %all-reduce.4.cloned.1.call-start = ((), (), s32[]{:S(2)}) async-start(), calls=%async_computation.2 | async-start | bytes 3145728 | tf_op jit(solution)/shard_map/psum | solution.py:194
  67.2 10.9 %copy-start.6 = (f32[512,768]{1,0:T(8,128)S(1)}, f32[512,768]{1,0:T(8,128)}, u32[]{:S(2)}) copy-start(f32[512,768]{1,0:T(8,128)} %copy-done.4) | copy-start | bytes 4718596
  67.2 10.9 %copy-start.16 = (bf16[768,768]{1,0:T(8,128)(2,1)S(1)}, bf16[768,768]{1,0:T(8,128)(2,1)}, u32[]{:S(2)}) copy-start(bf16[768,768]{1,0:T(8,128)(2,1)} %param.32) | copy-start | bytes 3538948
  88.9 16.0 %copy-start.14 = (f32[2,1]{0,1:T(1,128)S(1)}, f32[2,1]{0,1:T(1,128)}, u32[]{:S(2)}) copy-start(f32[2,1]{0,1:T(1,128)} %param.23) | copy-start | bytes 28
  98.2 95.8 %all-gather.11.cloned.1.call-start = ((), (), s32[]{:S(2)}) async-start(), calls=%async_computation.5 | async-start | bytes 4718592 | tf_op jit(solution)/shard_map/all_gather | solution.py:166
  119.9 3.3 copy-start.2
  119.9 3.8 %copy-start.9 = (bf16[1,1024,768]{2,1,0:T(8,128)(2,1)S(1)}, bf16[1,1024,768]{2,1,0:T(8,128)(2,1)}, u32[]{:S(2)}) copy-start(bf16[1,1024,768]{2,1,0:T(8,128)(2,1)} %all-reduce.4.cloned.1.call-done) | copy-start | bytes 4718596
  123.7 0.8 copy-start.18
  174.0 3.2 collective-permute-start
  179.4 1.2 copy-start.7
  183.4 83.4 %all-reduce.6.cloned.1.call-start = ((), (), s32[]{:S(2)}) async-start(), calls=%async_computation.3 | async-start | bytes 3145728 | tf_op jit(solution)/shard_map/psum | solution.py:194
  214.4 10.9 %copy-start.8 = (f32[512,768]{1,0:T(8,128)S(1)}, f32[512,768]{1,0:T(8,128)}, u32[]{:S(2)}) copy-start(f32[512,768]{1,0:T(8,128)} %copy-done.7) | copy-start | bytes 4718596
  214.4 10.9 %copy-start.17 = (bf16[768,768]{1,0:T(8,128)(2,1)S(1)}, bf16[768,768]{1,0:T(8,128)(2,1)}, u32[]{:S(2)}) copy-start(bf16[768,768]{1,0:T(8,128)(2,1)} %param.32) | copy-start | bytes 3538948
  266.7 3.3 copy-start.3
  266.7 3.8 %copy-start.10 = (bf16[1,1024,768]{2,1,0:T(8,128)(2,1)S(1)}, bf16[1,1024,768]{2,1,0:T(8,128)(2,1)}, u32[]{:S(2)}) copy-start(bf16[1,1024,768]{2,1,0:T(8,128)(2,1)} %all-reduce.6.cloned.1.call-done) | copy-start | bytes 4718596
  271.3 53.4 %copy-start.1 = (bf16[768,1536]{1,0:T(8,128)(2,1)S(1)}, bf16[768,1536]{1,0:T(8,128)(2,1)}, u32[]{:S(2)}) copy-start(bf16[768,1536]{1,0:T(8,128)(2,1)} %param.31) | copy-start | bytes 7077892
Sparse Core Ops, SparseCore 0:
  30.4 14.8 all-gather.8
  98.4 21.5 all-reduce.3
  183.5 10.5 all-gather.10
  245.1 21.5 all-reduce.5
